TPU v7x, 32 devices: a whole 2x2x4 slice. The times are simulated.
32 devices in a mesh: circ: 8 (over z, x), cell: 4 (over y, core).
Axes of the slice: x: 2, y: 2, z: 4, core: 2. Of those that a mesh axis runs over, the one named last changes fastest.
Arguments:
- flow_state: bfloat16 [35, 8, 16, 1024], P(None, 'circ', 'cell'), may hold values from -6 to 6
- time_coef: float32 [8, 16, 1024], P('circ', 'cell'), may hold values from 0.3 to 3
- axial_damp: bfloat16 [8, 16, 1024], P('circ', 'cell'), may hold values from 0.19921875 to 2
- plane_damp: bfloat16 [8, 16, 2048], P('circ', 'cell'), may hold values from 0.19921875 to 2
- periodic_damp: bfloat16 [8, 16, 64], P('circ', 'cell'), may hold values from 0.19921875 to 2
- flux_jacobian: float32 [3, 5, 5], replicated, may hold values from -2.5 to 2.5
- face_cells: int32 [2, 2048], replicated, may hold values from 0 to 1023, as said below
- periodic_cells: int32 [2, 64], replicated, may hold values from 0 to 1023, as said below
- face_map: int32 [64], replicated, may hold values from 0 to 63, each once
- wall_cells: int32 [1024], P('cell'), may hold values from 0 to 4095, as said below
- wall_normals: float32 [3, 1024], P(None, 'cell'), may hold values from -6 to 6
- pressure_weights: float32 [5], replicated, may hold values from -4 to 4
- mode_shapes: float32 [2, 8, 3, 400], replicated, may hold values from -0.00390625 to 0.00390625
Outputs:
- jacobian_image: bfloat16 [35, 8, 16, 1024], P(None, 'circ', 'cell')
- modal_forces: float32 [7, 400], replicated
Inputs may be any that keep to these rules, and one draw needn't show every extreme that they name: `face_cells`: each column names the two cells of a layer that one in-plane face joins; the two differ. `periodic_cells`: all 128 entries differ. `face_map`: each value of 0 to 63 once. `wall_cells`: an entry is the wall cell's layer within its cell block times 1024 plus its cell in the layer; entries may repeat.
All inputs are finite; a program needn't handle non-finite values.
Results may differ from a plain program's by a relative error of at most 0.0055.
Values may be sent and summed in bfloat16 or wider, within the bound.
A program may use at most 64 MiB of HBM per device.

v0:
```python
import math

import jax
import jax.numpy as jnp
import numpy as np
from jax import lax
from jax.sharding import PartitionSpec as P

NV = 5
HB = 7


def shifted(value, axis, steps):
    count = lax.axis_size(axis)
    first, last = (max(0, -steps), min(count, count - steps))
    return lax.ppermute(value, axis, [(source, source + steps) for source in range(first, last)])


def shifted_2(value, axis, steps):
    count = lax.axis_size(axis)
    pairs = [(source, (source + steps) % count) for source in range(count)]
    return lax.ppermute(value, axis, pairs)


def harmonic_matrix(instances):
    matrix_table = np.zeros((instances, instances))
    for row_index in range(instances):
        for column_index in range(instances):
            if row_index != column_index:
                offset_steps = row_index - column_index
                matrix_table[row_index, column_index] = (
                    0.5 * (-1.0) ** offset_steps / math.sin(math.pi * offset_steps / instances)
                )
    return matrix_table


def face_flux(jacobian, damping, lower_state, upper_state):
    total_state = lower_state + upper_state
    jump_state = upper_state - lower_state
    convected = jnp.einsum(
        "vw,nw...->nv...", jacobian, total_state, precision=lax.Precision.HIGHEST
    )
    return 0.5 * convected - 0.5 * damping * jump_state


def column_table(index_list, count):
    return (lax.iota(jnp.int32, count)[:, None] == index_list[None, :]).astype(jnp.bfloat16)


def take_columns(values, table):
    leading = values.shape[:-1]
    flat_values = values.reshape(-1, values.shape[-1])
    picked = jnp.dot(flat_values, table, preferred_element_type=jnp.float32)
    return picked.reshape(leading + (table.shape[1],))


def spread_columns(terms, table):
    leading = terms.shape[:-1]
    flat_terms = terms.reshape(-1, terms.shape[-1])
    high_part = flat_terms.astype(jnp.bfloat16)
    rest_one = flat_terms - high_part.astype(jnp.float32)
    middle_part = rest_one.astype(jnp.bfloat16)
    low_part = (rest_one - middle_part.astype(jnp.float32)).astype(jnp.bfloat16)
    contract = (((1,), (1,)), ((), ()))
    spread = lax.dot_general(high_part, table, contract, preferred_element_type=jnp.float32)
    spread = spread + lax.dot_general(
        middle_part, table, contract, preferred_element_type=jnp.float32
    )
    spread = spread + lax.dot_general(low_part, table, contract, preferred_element_type=jnp.float32)
    return spread.reshape(leading + (table.shape[0],))


def project_all(all_forces, mode_shapes, passages, angle_step, diameters):
    phase_index = (diameters[:, None] * diameters[None, :] % passages).astype(jnp.float32)
    cosine_table = jnp.cos(angle_step * phase_index)
    sine_table = jnp.sin(angle_step * phase_index)
    real_part = jnp.einsum("dp,pkn->dkn", cosine_table, all_forces, precision=lax.Precision.HIGHEST)
    imag_part = -jnp.einsum("dp,pkn->dkn", sine_table, all_forces, precision=lax.Precision.HIGHEST)
    return jnp.einsum(
        "dkm,dkn->nm", mode_shapes[0], real_part, precision=lax.Precision.HIGHEST
    ) + jnp.einsum("dkm,dkn->nm", mode_shapes[1], imag_part, precision=lax.Precision.HIGHEST)


def shards(
    flow_state,
    time_coef,
    axial_damp,
    plane_damp,
    periodic_damp,
    flux_jacobian,
    face_cells,
    periodic_cells,
    face_map,
    wall_cells,
    wall_normals,
    pressure_weights,
    mode_shapes,
):
    layers = flow_state.shape[2]
    plane_cells = flow_state.shape[3]
    passages = lax.axis_size("circ")
    state_narrow = flow_state.reshape(HB, NV, layers, plane_cells)
    current = state_narrow.astype(jnp.float32)
    harmonic = jnp.asarray(harmonic_matrix(HB), jnp.float32)
    jacobian_sum = time_coef[0][None, None] * jnp.einsum(
        "nm,mvac->nvac", harmonic, current, precision=lax.Precision.HIGHEST
    )
    cell_ids = lax.iota(jnp.int32, plane_cells)[:, None]
    owner_hits = cell_ids == face_cells[0][None, :]
    neighbour_hits = cell_ids == face_cells[1][None, :]
    owner_table = owner_hits.astype(jnp.bfloat16)
    neighbour_table = neighbour_hits.astype(jnp.bfloat16)
    signed_table = (owner_hits.astype(jnp.int32) - neighbour_hits.astype(jnp.int32)).astype(
        jnp.bfloat16
    )
    owner_values = take_columns(state_narrow, owner_table)
    neighbour_values = take_columns(state_narrow, neighbour_table)
    plane_flux = face_flux(
        flux_jacobian[1], plane_damp[0].astype(jnp.float32), owner_values, neighbour_values
    )
    jacobian_sum = jacobian_sum + spread_columns(plane_flux, signed_table)
    above_layer = shifted(state_narrow[:, :, :1], "cell", -1)
    upper_rows = jnp.concatenate([current[:, :, 1:], above_layer.astype(jnp.float32)], axis=2)
    own_flux = face_flux(flux_jacobian[0], axial_damp[0].astype(jnp.float32), current, upper_rows)
    zero_layer = jnp.zeros((HB, NV, 1, plane_cells), jnp.float32)
    jacobian_sum = (
        jacobian_sum + own_flux - jnp.concatenate([zero_layer, own_flux[:, :, :-1]], axis=2)
    )
    from_below = shifted(own_flux[:, :, -1:].astype(jnp.bfloat16), "cell", 1).astype(jnp.float32)
    jacobian_sum = jacobian_sum - jnp.concatenate(
        [from_below, jnp.zeros((HB, NV, layers - 1, plane_cells), jnp.float32)], axis=2
    )
    lower_side = periodic_cells[0]
    upper_side = periodic_cells[1]
    targets = lower_side[face_map]
    upper_table = column_table(upper_side, plane_cells)
    target_table = column_table(targets, plane_cells)
    own_targets = take_columns(state_narrow, target_table)
    own_upper = take_columns(state_narrow, upper_table)
    next_lower = shifted_2(own_targets.astype(jnp.bfloat16), "circ", -1)
    matched_next = next_lower.astype(jnp.float32)
    periodic_own = face_flux(
        flux_jacobian[2], periodic_damp[0].astype(jnp.float32), own_upper, matched_next
    )
    from_previous = shifted_2(periodic_own.astype(jnp.bfloat16), "circ", 1).astype(
        periodic_own.dtype
    )
    side_terms = jnp.concatenate([periodic_own, -from_previous], axis=3)
    side_table = jnp.concatenate([upper_table, target_table], axis=1)
    jacobian_sum = jacobian_sum + spread_columns(side_terms, side_table)
    jacobian_image = jacobian_sum.astype(jnp.bfloat16).reshape(HB * NV, 1, layers, plane_cells)
    flat_state = state_narrow.reshape(HB, NV, layers * plane_cells)
    wall_table = column_table(wall_cells, layers * plane_cells)
    wall_state = take_columns(flat_state, wall_table)
    wall_pressure = jnp.einsum(
        "v,nvw->nw", pressure_weights, wall_state, precision=lax.Precision.HIGHEST
    )
    block_force = jnp.einsum(
        "kw,nw->kn", wall_normals, wall_pressure, precision=lax.Precision.HIGHEST
    )
    angle_step = 2.0 * math.pi / passages
    diameters = lax.iota(jnp.int32, passages)
    passage_force = lax.psum(block_force, "cell")
    all_forces = lax.all_gather(passage_force[None], "circ", axis=0, tiled=True)
    modal_forces = project_all(all_forces, mode_shapes, passages, angle_step, diameters)
    return (jacobian_image, modal_forces)


def solution(mesh):
    placed = (
        P(None, "circ", "cell", None),
        P("circ", "cell", None),
        P("circ", "cell", None),
        P("circ", "cell", None),
        P("circ", "cell", None),
        P(),
        P(),
        P(),
        P(),
        P("cell"),
        P(None, "cell"),
        P(),
        P(),
    )
    return jax.shard_map(
        shards,
        mesh=mesh,
        in_specs=placed,
        out_specs=(P(None, "circ", "cell", None), P()),
        check_vma=False,
    )
```

profile of v0, /device:TPU:0, one launch (start us, length us, event | category | flops | bytes accessed | tf_op | source)
XLA Modules:
  0.0 92.0 jit_solution(8377886405390207188)
XLA Ops:
  0.7 1.1 %reshape_reshape.2 = bf16[140,1024]{1,0:T(8,128)(2,1)S(1)} reshape(bf16[35,1,4,1024]{3,2,1,0:T(4,128)(2,1)} %param.14) | data formatting | bytes 573440 | tf_op jit(solution)/shard_map/reshape;reshape | solution.py:52
  1.8 0.8 slice_bitcast_fusion.1
  2.5 0.7 compare_select_fusion
  3.2 0.8 gather_fusion
  4.4 0.6 copy.68
  5.0 6.0 %collective-permute-start.2 = (bf16[7,5,4,64]{3,1,2,0:T(8,128)(2,1)}, bf16[7,5,4,64]{3,1,2,0:T(8,128)(2,1)}, u32[]{:S(2)}, u32[]{:S(2)}) collective-permute-start(bf16[7,5,4,64]{3,1,2,0:T(8,128)(2,1)} %copy.68), channel_id=1, source_target_pairs={{0,28},{4,0},{8,4},{12,8},{16,12},{20,16},{24,20},{28,24},{1,29},{... | collective-permute-start | bytes 53768 | tf_op jit(solution)/shard_map/ppermute | solution.py:22
  11.1 0.7 copy.134
  11.8 1.3 %collective-permute-start = (bf16[7,5,1,1024]{3,0,2,1:T(8,128)(2,1)}, bf16[7,5,1,1024]{3,0,2,1:T(8,128)(2,1)}, u32[]{:S(2)}, u32[]{:S(2)}) collective-permute-start(bf16[7,5,1,1024]{3,0,2,1:T(8,128)(2,1)} %copy.134), channel_id=1, source_target_pairs={{1,0},{2,1},{3,2},{5,4},{6,5},{7,6},{9,8},{10,9},{11,10},{13,12},{... | collective-permute-start | bytes 215048 | tf_op jit(solution)/shard_map/ppermute | solution.py:16
  13.1 1.7 %fusion = f32[2048,140]{0,1:T(8,128)S(1)} fusion(bf16[140,1024]{1,0:T(8,128)(2,1)S(1)} %reshape_reshape.2, s32[2048]{0:T(1024)S(1)} %bitcast.128), kind=kOutput, calls=%fused_computation.3 | convolution fusion | flops 589299712 | bytes 1441792 | tf_op jit(solution)/shard_map/dot_general | solution.py:53
  14.8 2.8 %add_bitcast_fusion = (f32[140,2048]{1,0:T(8,128)S(1)}, f32[140,2048]{1,0:T(8,128)}) fusion(f32[2048,140]{0,1:T(8,128)S(1)} %fusion, bf16[140,1024]{1,0:T(8,128)(2,1)S(1)} %reshape_reshape.2, s32[2048]{0:T(1024)S(1)} %bitcast.124), kind=kOutput, calls=%fused_computation.36 | convolution fusion | flops 589873152 | bytes 3735552 | tf_op jit(solution)/shard_map/dot_general | solution.py:53
  17.9 1.8 %sub.47 = f32[7,5,4,2048]{3,2,1,0:T(4,128)S(1)} reshape(f32[140,2048]{1,0:T(8,128)} %get-tuple-element.7) | data formatting | bytes 2293760 | tf_op jit(solution)/shard_map/sub | solution.py:39
  19.8 0.6 fusion.77
  20.4 3.0 %fusion.15 = f32[7,5,4,2048]{3,1,2,0:T(8,128)S(1)} fusion(f32[7,5,4,2048]{3,2,1,0:T(4,128)S(1)} %sub.47, f32[7,5,4,2048]{3,2,1,0:T(4,128)S(1)} %add.64, f32[4,2048]{1,0:T(4,128)S(1)} %multiply_bitcast_fusion, f32[1,5,5]{2,0,1:T(1,128)S(1)} %get-tuple-element.10), kind=kOutput, calls=%fused_computation.21 | convolution fusion | flops 18063360 | bytes 3473508 | tf_op jit(solution)/shard_map/vw,nw...->nv.../dot_general | solution.py:40
  23.4 0.7 copy.55
  24.5 3.4 %fusion.2 = f32[140,1024]{1,0:T(8,128)} fusion(s32[2048]{0:T(1024)S(1)} %bitcast.129, s32[2048]{0:T(1024)S(1)} %bitcast.125, f32[140,2048]{1,0:T(8,128)S(1)} %reshape.68), kind=kOutput, calls=%fused_computation.6 | convolution fusion | flops 601792512 | bytes 1736704 | tf_op jit(solution)/shard_map/dot_general | solution.py:69
  28.0 3.4 %fusion.3 = f32[140,1024]{1,0:T(8,128)} fusion(s32[2048]{0:T(1024)S(1)} %bitcast.130, s32[2048]{0:T(1024)S(1)} %bitcast.126, f32[140,2048]{1,0:T(8,128)S(1)} %reshape.68), kind=kOutput, calls=%fused_computation.7 | convolution fusion | flops 600932352 | bytes 1736704 | tf_op jit(solution)/shard_map/dot_general | solution.py:66
  32.2 0.8 fusion.25
  33.4 8.5 %psum.7 = f32[1,3,7]{2,1,0:T(4,128)S(1)} all-reduce(f32[1,3,7]{2,1,0:T(4,128)S(1)} %convolution_bitcast_fusion.3), channel_id=1, replica_groups=mesh['circ'=8,'cell'=4] {'cell'}, use_global_device_ids=true, to_apply=%region_0.0 | all-reduce | flops 21 | bytes 168 | tf_op jit(solution)/shard_map/psum | solution.py:163
  41.9 26.3 %all_gather.3 = f32[8,3,7]{2,1,0:T(4,128)S(1)} all-gather(f32[1,3,7]{2,1,0:T(4,128)S(1)} %psum.7), channel_id=1, replica_groups=mesh['circ'=8,'cell'=4] {'circ'}, dimensions={0}, use_global_device_ids=true | all-gather | bytes 756 | tf_op jit(solution)/shard_map/all_gather | solution.py:164
  68.7 3.9 %fusion.22 = f32[140,1024]{1,0:T(8,128)S(1)} fusion(f32[140,1024]{1,0:T(8,128)} %fusion.2, f32[140,1024]{1,0:T(8,128)} %fusion.3, s32[2048]{0:T(1024)S(1)} %bitcast.131, s32[2048]{0:T(1024)S(1)} %bitcast.127, f32[140,2048]{1,0:T(8,128)S(1)} %reshape.68), kind=kOutput, calls=%fused_computation.32 | convolution fusion | flops 600358912 | bytes 2883584 | tf_op jit(solution)/shard_map/dot_general | solution.py:65
  72.8 0.8 fusion.27
  73.8 1.1 %fusion.78 = (bf16[7,5,4,64]{3,1,2,0:T(8,128)(2,1)S(1)}, f32[7,5,4,64]{3,1,2,0:T(8,128)S(1)}) fusion(f32[7,5,4,64]{3,2,1,0:T(4,128)S(1)} %reshape.70, bf16[7,5,4,64]{3,1,2,0:T(8,128)(2,1)} %collective-permute-done.2, f32[4,64]{1,0:T(4,128)S(1)} %multiply_bitcast_fusion.2, f32[1,5,5]{2,0,1:T(1,128)S(1)} %copy-done.3), kind=kOutput, calls=%fused_computation.123 | convolution fusion | flops 609280 | bytes 108644 | tf_op jit(solution)/shard_map/vw,nw...->nv.../dot_general | solution.py:40
  75.6 6.3 %collective-permute-done.3 = bf16[7,5,4,64]{3,1,2,0:T(8,128)(2,1)S(1)} collective-permute-done((bf16[7,5,4,64]{3,1,2,0:T(8,128)(2,1)S(1)}, bf16[7,5,4,64]{3,1,2,0:T(8,128)(2,1)S(1)}, u32[]{:S(2)}, u32[]{:S(2)}) %collective-permute-start.3) | collective-permute-done | bytes 17952 | tf_op jit(solution)/shard_map/ppermute | solution.py:22
  82.9 1.0 %copy.61 = f32[7,5,1,1024]{3,2,1,0:T(1,128)S(1)} copy(bf16[7,5,1,1024]{3,0,2,1:T(8,128)(2,1)} %collective-permute-done) | data formatting | bytes 215040 | tf_op jit(solution)/shard_map/convert_element_type | solution.py:123
  84.2 1.2 %fusion.28 = f32[7,4,1024,5]{2,3,1,0:T(8,128)S(1)} fusion(f32[7,5,4,1024]{3,2,1,0:T(4,128)S(1)} %bitcast.117, f32[1,5,5]{2,0,1:T(1,128)S(1)} %get-tuple-element.11), kind=kOutput, calls=%fused_computation.49 | convolution fusion | flops 8601600 | bytes 1146980 | tf_op jit(solution)/shard_map/vw,nw...->nv.../dot_general | solution.py:40
  85.4 0.9 convert_element_type.116
  86.3 0.5 fusion.34
  86.8 0.6 slice.70
  87.5 1.4 %collective-permute-start.1 = (bf16[7,5,1,1024]{3,0,2,1:T(8,128)(2,1)}, bf16[7,5,1,1024]{3,0,2,1:T(8,128)(2,1)S(1)}, u32[]{:S(2)}, u32[]{:S(2)}) collective-permute-start(bf16[7,5,1,1024]{3,0,2,1:T(8,128)(2,1)} %slice.70), channel_id=1, source_target_pairs={{0,1},{1,2},{2,3},{4,5},{5,6},{6,7},{8,9},{9,10},{10,11},{12,13},{... | collective-permute-start | bytes 215048 | tf_op jit(solution)/shard_map/ppermute | solution.py:16
  89.5 0.5 collective-permute-done.1
  90.0 1.1 %fusion.35 = bf16[7,5,4,1024]{3,0,2,1:T(8,128)(2,1)S(1)} fusion(f32[7,5,4,1024]{3,2,1,0:T(4,128)S(1)} %reshape.72, f32[7,5,4,1024]{3,0,2,1:T(8,128)S(1)} %fusion.34, f32[7,5,4,1024]{3,2,1,0:T(4,128)S(1)} %reshape.69, f32[7,7,1,1]{1,0,3,2:T(8,128)S(1)} %copy-done.13, f32[7,5,3,1024]{3,0,2,1:T(8,128)S(1)} %slice.57, ...), kind=kOutput, calls=%fused_computation.57 | convolution fusion | flops 13189120 | bytes 2812100 | tf_op jit(solution)/shard_map/nm,mvac->nvac/dot_general | solution.py:105
  91.1 1.0 %copy.74 = bf16[7,5,4,1024]{3,2,1,0:T(4,128)(2,1)} copy(bf16[7,5,4,1024]{3,0,2,1:T(8,128)(2,1)S(1)} %fusion.35) | data formatting | bytes 573440 | tf_op jit(solution)/shard_map/convert_element_type | solution.py:151
  (74 shorter events, 5.6 us)
Async XLA Ops:
  0.6 32.6 %copy-start = (f32[3,256]{1,0:T(4,128)S(1)}, f32[3,256]{1,0:T(4,128)}, u32[]{:S(2)}) copy-start(f32[3,256]{1,0:T(4,128)} %param.24) | copy-start | bytes 9220
  0.6 10.4 %copy-start.1 = (bf16[35,1,4,1024]{3,2,1,0:T(4,128)(2,1)S(1)}, bf16[35,1,4,1024]{3,2,1,0:T(4,128)(2,1)}, u32[]{:S(2)}) copy-start(bf16[35,1,4,1024]{3,2,1,0:T(4,128)(2,1)} %param.14) | copy-start | bytes 860164
  0.7 12.4 %copy-start.6 = (s32[2,2048]{1,0:T(2,128)S(1)}, s32[2,2048]{1,0:T(2,128)}, u32[]{:S(2)}) copy-start(s32[2,2048]{1,0:T(2,128)} %param.20) | copy-start | bytes 49156
  5.0 68.8 %collective-permute-start.2 = (bf16[7,5,4,64]{3,1,2,0:T(8,128)(2,1)}, bf16[7,5,4,64]{3,1,2,0:T(8,128)(2,1)}, u32[]{:S(2)}, u32[]{:S(2)}) collective-permute-start(bf16[7,5,4,64]{3,1,2,0:T(8,128)(2,1)} %copy.68), channel_id=1, source_target_pairs={{0,28},{4,0},{8,4},{12,8},{16,12},{20,16},{24,20},{28,24},{1,29},{... | collective-permute-start | bytes 53768 | tf_op jit(solution)/shard_map/ppermute | solution.py:22
  11.8 71.1 %collective-permute-start = (bf16[7,5,1,1024]{3,0,2,1:T(8,128)(2,1)}, bf16[7,5,1,1024]{3,0,2,1:T(8,128)(2,1)}, u32[]{:S(2)}, u32[]{:S(2)}) collective-permute-start(bf16[7,5,1,1024]{3,0,2,1:T(8,128)(2,1)} %copy.134), channel_id=1, source_target_pairs={{1,0},{2,1},{3,2},{5,4},{6,5},{7,6},{9,8},{10,9},{11,10},{13,12},{... | collective-permute-start | bytes 215048 | tf_op jit(solution)/shard_map/ppermute | solution.py:16
  13.1 14.9 %copy-start.8 = (s32[1,2048]{1,0:T(1,128)}, s32[1,2048]{1,0:T(1,128)S(1)}, u32[]{:S(2)}) copy-start(s32[1,2048]{1,0:T(1,128)S(1)} %get-tuple-element.8) | copy-start | bytes 24580
  13.1 14.9 %copy-start.10 = (s32[1,2048]{1,0:T(1,128)}, s32[1,2048]{1,0:T(1,128)S(1)}, u32[]{:S(2)}) copy-start(s32[1,2048]{1,0:T(1,128)S(1)} %get-tuple-element.9) | copy-start | bytes 24580
  17.6 2.2 %copy-start.12 = (f32[3,5,5]{2,0,1:T(4,128)S(1)}, f32[3,5,5]{2,0,1:T(4,128)}, u32[]{:S(2)}) copy-start(f32[3,5,5]{2,0,1:T(4,128)} %param.19) | copy-start | bytes 904
  17.6 2.8 %copy-start.5 = (bf16[1,4,2048]{2,1,0:T(4,128)(2,1)S(1)}, bf16[1,4,2048]{2,1,0:T(4,128)(2,1)}, u32[]{:S(2)}) copy-start(bf16[1,4,2048]{2,1,0:T(4,128)(2,1)} %param.17) | copy-start | bytes 49156
  31.4 0.8 copy-start.16
  31.8 1.2 %copy-start.15 = (f32[5]{0:T(128)S(1)}, f32[5]{0:T(128)}, u32[]{:S(2)}) copy-start(f32[5]{0:T(128)} %param.25) | copy-start | bytes 64
  31.8 36.8 %copy-start.9 = (s32[1,2048]{1,0:T(1,128)S(1)}, s32[1,2048]{1,0:T(1,128)}, u32[]{:S(2)}) copy-start(s32[1,2048]{1,0:T(1,128)} %copy-done.8) | copy-start | bytes 24580
  31.8 36.8 %copy-start.11 = (s32[1,2048]{1,0:T(1,128)S(1)}, s32[1,2048]{1,0:T(1,128)}, u32[]{:S(2)}) copy-start(s32[1,2048]{1,0:T(1,128)} %copy-done.10) | copy-start | bytes 24580
  68.6 4.0 %copy-start.2 = (f32[2,8,3,400]{3,1,2,0:T(8,128)S(1)}, f32[2,8,3,400]{3,1,2,0:T(8,128)}, u32[]{:S(2)}) copy-start(f32[2,8,3,400]{3,1,2,0:T(8,128)} %param.26) | copy-start | bytes 230404
  68.6 5.0 %copy-start.14 = (bf16[1,4,64]{2,1,0:T(4,128)(2,1)S(1)}, bf16[1,4,64]{2,1,0:T(4,128)(2,1)}, u32[]{:S(2)}) copy-start(bf16[1,4,64]{2,1,0:T(4,128)(2,1)} %param.18) | copy-start | bytes 1540
  68.7 5.1 %copy-start.3 = (f32[1,5,5]{2,0,1:T(1,128)S(1)}, f32[1,5,5]{2,0,1:T(1,128)}, u32[]{:S(2)}) copy-start(f32[1,5,5]{2,0,1:T(1,128)} %get-tuple-element.12) | copy-start | bytes 304
  68.7 6.3 %copy-start.7 = (bf16[1,4,1024]{2,1,0:T(4,128)(2,1)S(1)}, bf16[1,4,1024]{2,1,0:T(4,128)(2,1)}, u32[]{:S(2)}) copy-start(bf16[1,4,1024]{2,1,0:T(4,128)(2,1)} %param.16) | copy-start | bytes 24580
  74.9 6.9 %collective-permute-start.3 = (bf16[7,5,4,64]{3,1,2,0:T(8,128)(2,1)S(1)}, bf16[7,5,4,64]{3,1,2,0:T(8,128)(2,1)S(1)}, u32[]{:S(2)}, u32[]{:S(2)}) collective-permute-start(bf16[7,5,4,64]{3,1,2,0:T(8,128)(2,1)S(1)} %get-tuple-element.15), channel_id=1, source_target_pairs={{0,4},{4,8},{8,12},{12,16},{16,20},{20,24},{24,28},{28,0},{1,5},{5... | collective-permute-start | bytes 53768 | tf_op jit(solution)/shard_map/ppermute | solution.py:22
  87.5 2.5 %copy-start.4 = (f32[1,4,1024]{2,1,0:T(4,128)S(1)}, f32[1,4,1024]{2,1,0:T(4,128)}, u32[]{:S(2)}) copy-start(f32[1,4,1024]{2,1,0:T(4,128)} %param.15) | copy-start | bytes 49156
  87.5 2.5 %copy-start.13 = (f32[7,7,1,1]{1,0,3,2:T(8,128)S(1)}, f32[7,7,1,1]{1,0,3,2:T(8,128)}, u32[]{:S(2)}) copy-start(f32[7,7,1,1]{1,0,3,2:T(8,128)} %constant.44) | copy-start | bytes 592
  87.5 2.5 %collective-permute-start.1 = (bf16[7,5,1,1024]{3,0,2,1:T(8,128)(2,1)}, bf16[7,5,1,1024]{3,0,2,1:T(8,128)(2,1)S(1)}, u32[]{:S(2)}, u32[]{:S(2)}) collective-permute-start(bf16[7,5,1,1024]{3,0,2,1:T(8,128)(2,1)} %slice.70), channel_id=1, source_target_pairs={{0,1},{1,2},{2,3},{4,5},{5,6},{6,7},{8,9},{9,10},{10,11},{12,13},{... | collective-permute-start | bytes 215048 | tf_op jit(solution)/shard_map/ppermute | solution.py:16
where the time goes:
time: 93.8 us; the launch traced here: 92 us
  blocking collectives  34.8 us (37%)
  matrix products  25.9 us (28%)
  local copies, waits for them, and re-layouts  11.9 us (13%)
  starting transfers between devices  8.76 us (9%)
  waiting for transfers between devices  6.82 us (7%)
  other arithmetic  2.79 us (3%)
  between operations  1.13 us (1%)
    all_gather x1, blocking collectives, shards(): all_forces = lax.all_gather(passage_force[None], 'circ', axis=0, tiled=True)  26.3 us
    psum x1, blocking collectives, shards(): passage_force = lax.psum(block_force, 'cell')  8.48 us
    ppermute x2, waiting for transfers between devices, shifted_2(): return lax.ppermute(value, axis, pairs)  6.32 us
    ppermute x2, starting transfers between devices, shifted_2(): return lax.ppermute(value, axis, pairs)  6.06 us
    dot_general x5, matrix products, take_columns(): picked = jnp.dot(flat_values, table, preferred_element_type=jnp.float32)  5.79 us
    dot_general x3, matrix products, face_flux(): jnp.einsum('vw,nw...->nv...', jacobian, total_state, precision=lax.Precis...  5.32 us
    dot_general x2, matrix products, spread_columns(): lax.dot_general(high_part, table, contract, preferred_element_type=jnp.fl...  4.29 us
    dot_general x2, matrix products, spread_columns(): lax.dot_general(low_part, table, contract, preferred_element_type=jnp.flo...  3.84 us
  transfers between devices with their start and end apart: 4, of which 2 were waited for; matrix products, arithmetic and copies ran while one was open for 32% of the time, Pallas kernels for 0%

commit v1 on v0

v1 whole, which is shorter than its diff:
```python
import functools
import math

import jax
import jax.numpy as jnp
import numpy as np
from jax import lax
from jax.experimental import pallas as pl
from jax.experimental.pallas import tpu as pltpu
from jax.sharding import PartitionSpec as P

NV = 5
HB = 7
F32 = jnp.float32
BF16 = jnp.bfloat16
HI = lax.Precision.HIGHEST
MESH = pl.DeviceIdType.MESH
NT = (((1,), (1,)), ((), ()))


def up_to(value, step):
    return -(-value // step) * step


def harmonic_matrix(instances):
    matrix = np.zeros((instances, instances))
    for n in range(instances):
        for m in range(instances):
            if n != m:
                matrix[n, m] = 0.5 * (-1.0) ** (n - m) / math.sin(math.pi * (n - m) / instances)
    return matrix


def constants(layers, passages, walls_k):
    rows = HB * NV * layers
    padded = up_to(rows, 16)
    side = up_to(HB * NV, 16)
    width = padded + 2 * side
    harmonic = harmonic_matrix(HB)
    mix = np.zeros((padded, padded), np.int32)
    axial = np.zeros((padded, width), np.int32)
    fixed = np.zeros((4, padded, width), np.float32)
    pick = np.zeros((2 * side, padded), np.float32)
    weights = np.zeros((8, padded), np.int32)
    variable = np.full((padded, 128), -1, np.int32)
    time = np.zeros((padded, width), np.float32)
    for i in range(rows):
        r, a = divmod(i, layers)
        n, v = divmod(r, NV)
        variable[i] = v
        weights[n, i] = v + 1
        if a == 0:
            pick[r, i] = 1
        if a == layers - 1:
            pick[side + r, i] = 1
        for w in range(NV):
            q = n * NV + w
            mix[i, q * layers + a] = w + 1
            axial[i, q * layers + a + 1 if a < layers - 1 else padded + q] = w + 1
            axial[i, q * layers + a - 1 if a > 0 else padded + side + q] = -(w + 1)
        fixed[2, i, i] = -1
        fixed[2, i, i + 1 if a < layers - 1 else padded + r] = 1
        fixed[3, i, i] = -1
        fixed[3, i, i - 1 if a > 0 else padded + side + r] = 1
        for m in range(HB):
            time[i, (m * NV + v) * layers + a] = harmonic[n, m]
    time_high = time.astype(BF16)
    fixed[0] = time_high.astype(np.float32)
    fixed[1] = time - fixed[0]
    lanes = up_to(walls_k * passages, 128)
    modes = np.zeros((lanes, 2 * passages * 8), np.float32)
    for p in range(passages):
        for d in range(passages):
            angle = 2.0 * math.pi * (d * p % passages) / passages
            for k in range(walls_k):
                modes[p * walls_k + k, d * 8 + k] = math.cos(angle)
                modes[p * walls_k + k, (passages + d) * 8 + k] = -math.sin(angle)
    return (
        mix,
        axial,
        fixed.reshape(4 * padded, width).astype(BF16),
        pick.astype(BF16),
        weights,
        variable,
        modes,
    )


def split(value):
    high = value.astype(BF16)
    return high, (value - high.astype(F32)).astype(BF16)


def dot(a, b):
    return jnp.dot(a, b, preferred_element_type=F32)


def kernel(
    state, time_coef, axial_damp, plane_damp, periodic_damp, jac, faces, sides, face_map,
    wall_cells, normals, press_w, mode_shapes,
    mix_c, axial_c, fixed_c, pick_c, weights_c, variable_c, modes_c,
    image, modal,
    extra, plus, signed, stack, cell_out, above, below, side_out, side_next, side_prev,
    forces_1, forces_2, shapes_pad, total,
    cell_send, cell_recv, side_send, side_recv, f1_send, f1_recv, f2_send, f2_recv,
    *, n_cell, n_circ, layers,
):
    me_cell = lax.axis_index("cell")
    me_circ = lax.axis_index("circ")

    def cell_at(j):
        return {"cell": lax.rem(me_cell + j, n_cell)}

    def circ_at(j):
        return {"circ": lax.rem(me_circ + j, n_circ)}

    barrier = pltpu.get_barrier_semaphore()
    for j in range(1, n_cell):
        pl.semaphore_signal(barrier, inc=1, device_id=cell_at(j), device_id_type=MESH)
    for j in range(1, n_circ):
        pl.semaphore_signal(barrier, inc=1, device_id=circ_at(j), device_id_type=MESH)

    padded, cells = state.shape
    n_faces = faces.shape[1]
    n_walls = wall_cells.shape[1]
    per = sides.shape[1]
    side_rows = above.shape[0]
    walls_k = normals.shape[0]
    groups = padded // 8

    def by_layer(value, pattern):
        return (value.reshape(groups, 8, value.shape[1]) * pattern[None]).reshape(value.shape)

    def pattern_of(rows):
        return jnp.concatenate([rows] * (8 // layers), axis=0)

    u = state[...]

    order = face_map[...]
    hits = (lax.broadcasted_iota(jnp.int32, (per, per), 0) == order).astype(F32)
    targets = jnp.dot(sides[0:1, :].astype(F32), hits, precision=HI, preferred_element_type=F32)
    targets = (targets + 0.5).astype(jnp.int32)
    wall_index = wall_cells[...]
    wall_layer = lax.div(wall_index, cells)
    wall_column = wall_index - wall_layer * cells
    columns = jnp.concatenate([wall_column, sides[1:2, :], targets], axis=1)
    chunk = 256
    step_rows = 16
    for q in range(cells // chunk):
        low = jnp.clip(columns - q * chunk, -1, chunk).astype(F32).astype(BF16)
        low = jnp.broadcast_to(low, (step_rows, low.shape[1]))

        def fill(i, carry, q=q, low=low):
            base = lax.broadcasted_iota(jnp.int32, low.shape, 0) + i * step_rows
            hit = base.astype(F32).astype(BF16) == low
            start = pl.multiple_of(q * chunk + i * step_rows, step_rows)
            extra[pl.ds(start, step_rows), :] = jnp.where(hit, 1.0, 0.0).astype(BF16)
            return carry

        lax.fori_loop(0, chunk // step_rows, fill, 0, unroll=4)

    cell_out[0 : 2 * side_rows, :] = dot(pick_c[...], u).astype(BF16)
    damp = axial_damp[0].astype(F32)
    last = damp[layers - 1 : layers]
    cell_out[2 * side_rows :, :] = jnp.broadcast_to(last, (16, cells)).astype(BF16)

    gathered = dot(u, extra[...])
    own_side = gathered[:, n_walls:]
    side_out[0:padded, :] = own_side.astype(BF16)
    side_damp = periodic_damp[0].astype(F32)
    side_pattern = pattern_of(jnp.concatenate([side_damp, side_damp], axis=1))
    side_out[padded:, :] = jnp.concatenate([side_pattern, side_pattern], axis=0).astype(BF16)

    layer_of = lax.rem(lax.broadcasted_iota(jnp.int32, (8, n_walls), 0), layers)
    here = by_layer(gathered[:, :n_walls], (layer_of == wall_layer).astype(F32))
    weight_class = weights_c[...]
    weight = jnp.zeros(weight_class.shape, F32)
    for v in range(NV):
        weight = jnp.where(weight_class == v + 1, press_w[v], weight)
    pressure = jnp.dot(weight, here, precision=HI, preferred_element_type=F32)
    force = lax.dot_general(pressure, normals[...], NT, precision=HI, preferred_element_type=F32)
    lanes = forces_1.shape[2]
    lane = lax.broadcasted_iota(jnp.int32, (8, lanes), 1)
    tile = jnp.zeros((8, lanes), F32)
    for k in range(walls_k):
        tile = jnp.where(lane == me_circ * walls_k + k, force[:, k : k + 1], tile)
    forces_1[me_cell] = tile

    variable = variable_c[...]

    def row_values(face):
        found = []
        for w in range(NV):
            value = jnp.zeros(variable.shape, F32)
            for v in range(NV):
                value = jnp.where(variable == v, 0.5 * jac[face, v, w], value)
            found.append(value)
        return found

    def mixing(face, classes, signs):
        values = row_values(face)
        pieces = []
        for start in range(0, classes.shape[1], 128):
            part = classes[:, start : start + 128]
            width = part.shape[1]
            value = jnp.zeros(part.shape, F32)
            for w in range(NV):
                value = jnp.where(part == w + 1, values[w][:, :width], value)
                if signs:
                    value = jnp.where(part == -(w + 1), -values[w][:, :width], value)
            pieces.append(value)
        return split(jnp.concatenate(pieces, axis=1))

    pl.semaphore_wait(barrier, n_cell - 1 + n_circ - 1)
    copies = []

    def send(source, target, send_sem, recv_sem, device):
        copy = pltpu.make_async_remote_copy(
            src_ref=source, dst_ref=target, send_sem=send_sem, recv_sem=recv_sem,
            device_id=device, device_id_type=MESH,
        )
        copy.start()
        copies.append(copy)
        return copy

    to_below = send(
        cell_out.at[pl.ds(0, side_rows)], above, cell_send.at[0], cell_recv.at[0],
        cell_at(n_cell - 1),
    )
    to_above = send(
        cell_out.at[pl.ds(side_rows, side_rows + 16)], below, cell_send.at[1], cell_recv.at[1],
        cell_at(1),
    )
    to_prev = send(side_out, side_next, side_send.at[0], side_recv.at[0], circ_at(n_circ - 1))
    to_next = send(side_out, side_prev, side_send.at[1], side_recv.at[1], circ_at(1))
    first = [
        send(forces_1.at[me_cell], forces_1.at[me_cell], f1_send.at[j], f1_recv.at[j], cell_at(j))
        for j in range(1, n_cell)
    ]

    mix_high, mix_low = mixing(1, mix_c[...], False)
    convected = (dot(mix_high, u) + dot(mix_low, u)).astype(BF16)
    for q in range(cells // chunk):
        ends = []
        for side in range(2):
            low = jnp.clip(faces[side : side + 1, :] - q * chunk, -1, chunk)
            low = low.astype(F32).astype(BF16)
            ends.append(jnp.broadcast_to(low, (step_rows, n_faces)))

        def build(i, carry, q=q, ends=ends):
            base = lax.broadcasted_iota(jnp.int32, (step_rows, n_faces), 0) + i * step_rows
            base = base.astype(F32).astype(BF16)
            one = jnp.ones((step_rows, n_faces), BF16)
            zero = jnp.zeros((step_rows, n_faces), BF16)
            owner = jnp.where(base == ends[0], one, zero)
            other = jnp.where(base == ends[1], one, zero)
            start = pl.multiple_of(q * chunk + i * step_rows, step_rows)
            plus[pl.ds(start, step_rows), :] = owner + other
            signed[pl.ds(start, step_rows), :] = owner - other
            return carry

        lax.fori_loop(0, chunk // step_rows, build, 0, unroll=2)

    for copy in first:
        copy.wait_recv()
    summed = forces_1[0]
    for j in range(1, n_cell):
        summed = summed + forces_1[j]
    forces_2[0] = summed

    plane_pattern = pattern_of(0.5 * plane_damp[0].astype(F32))
    flux = dot(convected, plus[...]) + by_layer(dot(u, signed[...]), plane_pattern)
    second = [
        send(forces_2.at[0], forces_2.at[j], f2_send.at[j], f2_recv.at[j], circ_at(j))
        for j in range(1, n_circ)
    ]
    total[...] = lax.dot_general(flux.astype(BF16), signed[...], NT, preferred_element_type=F32)

    shapes_pad[...] = jnp.zeros_like(shapes_pad)
    for part in range(2):
        for d in range(n_circ):
            at = (part * n_circ + d) * 8
            shapes_pad[at : at + walls_k, :] = mode_shapes[part, d]
    by_passage = jnp.dot(modes_c[...], shapes_pad[...], precision=HI, preferred_element_type=F32)

    axial_high, axial_low = mixing(0, axial_c[...], True)
    to_below.wait_recv()
    to_above.wait_recv()
    stack[0:padded, :] = u
    above_rows = above[...].astype(F32)
    stack[padded : padded + side_rows, :] = jnp.where(
        me_cell == n_cell - 1, 0.0, above_rows
    ).astype(BF16)
    below_rows = below[0:side_rows, :].astype(F32)
    stack[padded + side_rows :, :] = jnp.where(
        me_cell == 0, -cell_out[0:side_rows, :].astype(F32), below_rows
    ).astype(BF16)
    below_damp = below[side_rows : side_rows + 16, :].astype(F32)[0:1]
    below_damp = jnp.where(me_cell == 0, 0.0, below_damp)
    held = stack[...]
    derived = dot(fixed_c[...], held)
    result = by_layer(
        derived[0:padded] + derived[padded : 2 * padded], pattern_of(time_coef[0])
    )
    result = result - by_layer(derived[2 * padded : 3 * padded], pattern_of(0.5 * damp))
    lower_damp = jnp.concatenate([below_damp, damp[0 : layers - 1]], axis=0)
    result = result - by_layer(derived[3 * padded :], pattern_of(0.5 * lower_damp))
    result = result + dot(axial_high, held) + dot(axial_low, held)

    side_high, side_low = mixing(2, mix_c[...], False)
    to_prev.wait_recv()
    to_next.wait_recv()
    left = lax.broadcasted_iota(jnp.int32, (padded, 2 * per), 1) < per
    ahead = pltpu.roll(side_next[0:padded, :].astype(F32), per, 1)
    back = pltpu.roll(side_prev[0:padded, :].astype(F32), per, 1)
    back_damp = side_prev[padded:, :].astype(F32)[0:8]
    lower = jnp.where(left, own_side, back)
    upper = jnp.where(left, ahead, own_side)
    side_s = 0.5 * jnp.where(left[0:8], side_pattern, back_damp)
    lower_b, upper_b = lower.astype(BF16), upper.astype(BF16)
    side_flux = dot(side_high, lower_b) + dot(side_high, upper_b)
    side_flux = side_flux + dot(side_low, lower_b) + dot(side_low, upper_b)
    side_flux = side_flux - by_layer(upper - lower, side_s)
    side_flux = jnp.where(left, side_flux, -side_flux).astype(BF16)
    result = result + lax.dot_general(
        side_flux, extra[:, n_walls:], NT, preferred_element_type=F32
    )
    image[...] = (result + total[...]).astype(BF16)

    for copy in second:
        copy.wait_recv()
    every = forces_2[0]
    for j in range(1, n_circ):
        every = every + forces_2[j]
    answer = jnp.dot(every, by_passage, precision=HI, preferred_element_type=F32)
    modal[...] = answer[0:HB]
    for copy in copies:
        copy.wait_send()


def shards(
    flow_state, time_coef, axial_damp, plane_damp, periodic_damp, flux_jacobian, face_cells,
    periodic_cells, face_map, wall_cells, wall_normals, pressure_weights, mode_shapes,
):
    layers, cells = flow_state.shape[2:]
    n_cell = lax.axis_size("cell")
    n_circ = lax.axis_size("circ")
    walls_k = wall_normals.shape[0]
    n_modes = mode_shapes.shape[3]
    per = face_map.shape[0]
    n_faces = face_cells.shape[1]
    n_walls = wall_cells.shape[0]
    fixed = constants(layers, n_circ, walls_k)
    rows = HB * NV * layers
    padded = fixed[0].shape[0]
    side = fixed[3].shape[0] // 2
    lanes = fixed[6].shape[0]
    state = jnp.pad(flow_state.reshape(rows, cells), ((0, padded - rows), (0, 0)))
    vmem = pl.BlockSpec(memory_space=pltpu.VMEM)
    smem = pl.BlockSpec(memory_space=pltpu.SMEM)
    dma = pltpu.SemaphoreType.DMA
    image, modal = pl.pallas_call(
        functools.partial(kernel, n_cell=n_cell, n_circ=n_circ, layers=layers),
        out_shape=(
            jax.ShapeDtypeStruct((padded, cells), BF16),
            jax.ShapeDtypeStruct((HB, n_modes), F32),
        ),
        in_specs=[vmem] * 5 + [smem] + [vmem] * 5 + [smem] + [vmem] * 8,
        out_specs=(vmem, vmem),
        scratch_shapes=[
            pltpu.VMEM((cells, n_walls + 2 * per), BF16),
            pltpu.VMEM((cells, n_faces), BF16),
            pltpu.VMEM((cells, n_faces), BF16),
            pltpu.VMEM((padded + 2 * side, cells), BF16),
            pltpu.VMEM((2 * side + 16, cells), BF16),
            pltpu.VMEM((side, cells), BF16),
            pltpu.VMEM((side + 16, cells), BF16),
            pltpu.VMEM((padded + 16, 2 * per), BF16),
            pltpu.VMEM((padded + 16, 2 * per), BF16),
            pltpu.VMEM((padded + 16, 2 * per), BF16),
            pltpu.VMEM((n_cell, 8, lanes), F32),
            pltpu.VMEM((n_circ, 8, lanes), F32),
            pltpu.VMEM((2 * n_circ * 8, n_modes), F32),
            pltpu.VMEM((padded, cells), F32),
            dma((2,)), dma((2,)), dma((2,)), dma((2,)),
            dma((n_cell,)), dma((n_cell,)), dma((n_circ,)), dma((n_circ,)),
        ],
        compiler_params=pltpu.CompilerParams(collective_id=0, has_side_effects=True),
    )(
        state, time_coef, axial_damp, plane_damp, periodic_damp, flux_jacobian, face_cells,
        periodic_cells, face_map[None], wall_cells[None], wall_normals, pressure_weights,
        mode_shapes, *fixed,
    )
    return image[:rows].reshape(HB * NV, 1, layers, cells), modal


def solution(mesh):
    circ = P("circ", "cell", None)
    placed = (
        P(None, "circ", "cell", None), circ, circ, circ, circ, P(), P(), P(), P(),
        P("cell"), P(None, "cell"), P(), P(),
    )
    return jax.shard_map(
        shards,
        mesh=mesh,
        in_specs=placed,
        out_specs=(P(None, "circ", "cell", None), P()),
        check_vma=False,
    )
```

time: 93.8 us -> 25.8 us (0.28); the launches traced: 92 us -> 25.5 us
  blocking collectives: 34.8 us -> 0 us
  matrix products: 25.9 us -> 0 us
  Pallas kernels: 0 us -> 17.8 us
  starting transfers between devices: 8.76 us -> 0 us
  waiting for transfers between devices: 6.82 us -> 0 us
  local copies, waits for them, and re-layouts: 11.9 us -> 7.08 us
  other arithmetic: 2.79 us -> 0 us
    all_gather x1 -> x0, blocking collectives: 26.3 us -> none  [shards(): all_forces = lax.all_gather(passage_force[None], 'circ', axis=0, tiled=True)]
    dot_general x21 -> x0, matrix products: 25.9 us -> none  [the longest x5 5.79 us: take_columns(): picked = jnp.dot(flat_values, table, preferred_element_type=jnp.float32)]
    pallas_call x0 -> x1, Pallas kernels: none -> 17.8 us  [shards(): pl.pallas_call(functools.partial(kernel, n_cell=n_cell, n_circ=n_circ, la...]
    ppermute x4 -> x0, starting transfers between devices: 8.76 us -> none  [the longest x2 6.06 us: shifted_2(): return lax.ppermute(value, axis, pairs)]
    psum x1 -> x0, blocking collectives: 8.48 us -> none  [shards(): passage_force = lax.psum(block_force, 'cell')]
    ppermute x4 -> x0, waiting for transfers between devices: 6.82 us -> none  [the longest x2 6.32 us: shifted_2(): return lax.ppermute(value, axis, pairs)]
    convert_element_type x5 -> x0, local copies, waits for them, and re-layouts: 2.74 us -> none  [the longest x1 1 us: shards(): above_layer.astype(jnp.float32)]
    sub x2 -> x0, local copies, waits for them, and re-layouts: 2.55 us -> none  [the longest x1 1.81 us: face_flux(): jump_state = upper_state - lower_state]
  transfers between devices with their start and end apart: 4 -> 0, of which waited for: 2 -> 0; matrix products, arithmetic and copies ran while one was open for 32% -> 0% of each run, Pallas kernels for 0% -> 0%
where the time goes in v1:
time: 25.8 us; the launch traced here: 25.5 us
  Pallas kernels  17.8 us (69%)
  local copies, waits for them, and re-layouts  7.08 us (27%)
  between operations  0.65 us (3%)
    pallas_call x1, Pallas kernels, shards(): pl.pallas_call(functools.partial(kernel, n_cell=n_cell, n_circ=n_circ, la...  17.8 us
    unnamed x5, local copies, waits for them, and re-layouts  3.53 us
    reshape x1, local copies, waits for them, and re-layouts, shards(): return (image[:rows].reshape(HB * NV, 1, layers, cells), modal)  1.8 us
    reshape x1, local copies, waits for them, and re-layouts, shards(): flow_state.reshape(rows, cells)  1.03 us
    pad x1, local copies, waits for them, and re-layouts, shards(): jnp.pad(flow_state.reshape(rows, cells), ((0, padded - rows), (0, 0)))  0.73 us

profile of v1, /device:TPU:0, one launch (start us, length us, event | category | flops | bytes accessed | tf_op | source)
XLA Modules:
  0.0 25.5 jit_solution(17704521481912340256)
XLA Ops:
  0.6 1.3 %copy.22.jac = f32[3,5,5]{2,1,0:T(8,128)} copy(f32[3,5,5]{2,0,1:T(4,128)} %param.25) | data formatting | bytes 600 | tf_op args[5]
  1.9 1.6 %copy.23.mode_shapes = f32[2,8,3,400]{3,2,1,0:T(4,128)} copy(f32[2,8,3,400]{3,1,2,0:T(8,128)} %param.32) | data formatting | bytes 153600 | tf_op args[12]
  3.5 1.0 %reshape.10 = bf16[140,1024]{1,0:T(8,128)(2,1)S(1)} reshape(bf16[35,1,4,1024]{3,2,1,0:T(4,128)(2,1)} %param.20) | data formatting | bytes 573440 | tf_op jit(solution)/shard_map/reshape | solution.py:358
  4.6 0.7 %pad.4.state = bf16[144,1024]{1,0:T(8,128)(2,1)} pad(bf16[140,1024]{1,0:T(8,128)(2,1)S(1)} %reshape.10, bf16[]{:T(256)} %constant.16.clone.1), padding=0_4x0_0 | pad | bytes 581634 | tf_op jit(solution)/shard_map/jit(_pad)/pad | solution.py:358
  5.3 17.8 %shard_map.203 = (bf16[144,1024]{1,0:T(8,128)(2,1)}, f32[7,400]{1,0:T(8,128)}) custom-call(bf16[144,1024]{1,0:T(8,128)(2,1)} %pad.4.state, f32[1,4,1024]{2,1,0:T(4,128)} %time_coef.1, bf16[1,4,1024]{2,1,0:T(4,128)(2,1)} %axial_damp.1, bf16[1,4,2048]{2,1,0:T(4,128)(2,1)} %plane_damp.1, bf16[1,4,64]{2,1,0:T(4,128)(2,1)} %periodic_damp.1, ...), custom_call_target="tpu_custom_call" | custom-call | tf_op jit(solution)/shard_map/pallas_call | solution.py:362
  23.1 0.0 copy-start
  23.1 1.8 %reshape.11 = bf16[35,1,4,1024]{3,2,0,1:T(4,128)(2,1)} reshape(bf16[140,1024]{1,0:T(8,128)(2,1)} %bitcast.4) | data formatting | bytes 573440 | tf_op jit(solution)/shard_map/reshape | solution.py:394
  24.9 0.0 copy-done
  24.9 0.6 %copy.26 = f32[7,400]{1,0:T(8,128)} copy(f32[7,400]{1,0:T(8,128)S(1)} %copy-done) | data formatting | bytes 22400
Async XLA Ops:
  23.1 1.8 %copy-start = (f32[7,400]{1,0:T(8,128)S(1)}, f32[7,400]{1,0:T(8,128)}, u32[]{:S(2)}) copy-start(f32[7,400]{1,0:T(8,128)} %get-tuple-element.11) | copy-start | bytes 33604

commit v2 on v1

--- a/solution.py
+++ b/solution.py
@@ -31,23 +31,34 @@
     return matrix
 
 
+def near_scale(values):
+    scales = 1.0 + np.arange(4096) / 4096.0
+    scaled = scales[:, None] * values[None, :]
+    rounded = scaled.astype(BF16).astype(np.float64)
+    return float(scales[np.argmin(np.max(np.abs(rounded / scaled - 1.0), axis=1))])
+
+
 def constants(layers, passages, walls_k):
     rows = HB * NV * layers
     padded = up_to(rows, 16)
     side = up_to(HB * NV, 16)
     width = padded + 2 * side
     harmonic = harmonic_matrix(HB)
-    mix = np.zeros((padded, padded), np.int32)
-    axial = np.zeros((padded, width), np.int32)
-    fixed = np.zeros((4, padded, width), np.float32)
+    scale = near_scale(np.unique(np.abs(harmonic[harmonic != 0])))
+    mix = np.zeros((padded, padded), np.float32)
+    axial = np.zeros((padded, width), np.float32)
+    fixed = np.zeros((3, padded, width), np.float32)
     pick = np.zeros((2 * side, padded), np.float32)
     weights = np.zeros((8, padded), np.int32)
-    variable = np.full((padded, 128), -1, np.int32)
-    time = np.zeros((padded, width), np.float32)
+    of_row = np.zeros((padded, NV), np.float32)
+    of_column = np.zeros((NV, width), np.float32)
     for i in range(rows):
         r, a = divmod(i, layers)
         n, v = divmod(r, NV)
-        variable[i] = v
+        of_row[i, v] = 1
+        of_column[v, i] = 1
+        of_column[v, padded + r] = 1
+        of_column[v, padded + side + r] = 1
         weights[n, i] = v + 1
         if a == 0:
             pick[r, i] = 1
@@ -55,40 +66,34 @@
             pick[side + r, i] = 1
         for w in range(NV):
             q = n * NV + w
-            mix[i, q * layers + a] = w + 1
-            axial[i, q * layers + a + 1 if a < layers - 1 else padded + q] = w + 1
-            axial[i, q * layers + a - 1 if a > 0 else padded + side + q] = -(w + 1)
+            mix[i, q * layers + a] = 1
+            axial[i, q * layers + a + 1 if a < layers - 1 else padded + q] = 1
+            axial[i, q * layers + a - 1 if a > 0 else padded + side + q] = -1
+        fixed[1, i, i] = -1
+        fixed[1, i, i + 1 if a < layers - 1 else padded + r] = 1
         fixed[2, i, i] = -1
-        fixed[2, i, i + 1 if a < layers - 1 else padded + r] = 1
-        fixed[3, i, i] = -1
-        fixed[3, i, i - 1 if a > 0 else padded + side + r] = 1
+        fixed[2, i, i - 1 if a > 0 else padded + side + r] = 1
         for m in range(HB):
-            time[i, (m * NV + v) * layers + a] = harmonic[n, m]
-    time_high = time.astype(BF16)
-    fixed[0] = time_high.astype(np.float32)
-    fixed[1] = time - fixed[0]
+            fixed[0, i, (m * NV + v) * layers + a] = scale * harmonic[n, m]
     lanes = up_to(walls_k * passages, 128)
-    modes = np.zeros((lanes, 2 * passages * 8), np.float32)
+    modes = np.zeros((lanes, 2 * walls_k * passages), np.float32)
     for p in range(passages):
         for d in range(passages):
             angle = 2.0 * math.pi * (d * p % passages) / passages
             for k in range(walls_k):
-                modes[p * walls_k + k, d * 8 + k] = math.cos(angle)
-                modes[p * walls_k + k, (passages + d) * 8 + k] = -math.sin(angle)
-    return (
+                modes[p * walls_k + k, k * passages + d] = math.cos(angle)
+                modes[p * walls_k + k, (walls_k + k) * passages + d] = -math.sin(angle)
+    arrays = (
         mix,
         axial,
-        fixed.reshape(4 * padded, width).astype(BF16),
+        fixed.reshape(3 * padded, width).astype(BF16),
         pick.astype(BF16),
         weights,
-        variable,
+        of_row.astype(BF16),
+        of_column.astype(BF16),
         modes,
     )
-
-
-def split(value):
-    high = value.astype(BF16)
-    return high, (value - high.astype(F32)).astype(BF16)
+    return arrays, scale
 
 
 def dot(a, b):
@@ -98,12 +103,12 @@
 def kernel(
     state, time_coef, axial_damp, plane_damp, periodic_damp, jac, faces, sides, face_map,
     wall_cells, normals, press_w, mode_shapes,
-    mix_c, axial_c, fixed_c, pick_c, weights_c, variable_c, modes_c,
+    mix_c, axial_c, fixed_c, pick_c, weights_c, of_row_c, of_column_c, modes_c,
     image, modal,
     extra, plus, signed, stack, cell_out, above, below, side_out, side_next, side_prev,
-    forces_1, forces_2, shapes_pad, total,
+    forces_1, forces_2, flux, total,
     cell_send, cell_recv, side_send, side_recv, f1_send, f1_recv, f2_send, f2_recv,
-    *, n_cell, n_circ, layers,
+    *, n_cell, n_circ, layers, padded, scale,
 ):
     me_cell = lax.axis_index("cell")
     me_circ = lax.axis_index("circ")
@@ -120,7 +125,7 @@
     for j in range(1, n_circ):
         pl.semaphore_signal(barrier, inc=1, device_id=circ_at(j), device_id_type=MESH)
 
-    padded, cells = state.shape
+    n_rows, _, cells = state.shape
     n_faces = faces.shape[1]
     n_walls = wall_cells.shape[1]
     per = sides.shape[1]
@@ -134,7 +139,10 @@
     def pattern_of(rows):
         return jnp.concatenate([rows] * (8 // layers), axis=0)
 
-    u = state[...]
+    wide = state[...].astype(F32)
+    pieces = [wide[r] for r in range(n_rows)]
+    pieces.append(jnp.zeros((padded - n_rows * layers, cells), F32))
+    u = jnp.concatenate(pieces, axis=0).astype(BF16)
 
     order = face_map[...]
     hits = (lax.broadcasted_iota(jnp.int32, (per, per), 0) == order).astype(F32)
@@ -186,30 +194,45 @@
         tile = jnp.where(lane == me_circ * walls_k + k, force[:, k : k + 1], tile)
     forces_1[me_cell] = tile
 
-    variable = variable_c[...]
-
-    def row_values(face):
-        found = []
-        for w in range(NV):
-            value = jnp.zeros(variable.shape, F32)
-            for v in range(NV):
-                value = jnp.where(variable == v, 0.5 * jac[face, v, w], value)
-            found.append(value)
-        return found
-
-    def mixing(face, classes, signs):
-        values = row_values(face)
-        pieces = []
-        for start in range(0, classes.shape[1], 128):
-            part = classes[:, start : start + 128]
-            width = part.shape[1]
-            value = jnp.zeros(part.shape, F32)
-            for w in range(NV):
-                value = jnp.where(part == w + 1, values[w][:, :width], value)
-                if signs:
-                    value = jnp.where(part == -(w + 1), -values[w][:, :width], value)
-            pieces.append(value)
-        return split(jnp.concatenate(pieces, axis=1))
+    def mixing(face, mask):
+        values = (0.5 * jac[:, face, :]).astype(BF16)
+        across = dot(values, of_column_c[:, : mask.shape[1]]).astype(BF16)
+        return (dot(of_row_c[...], across) * mask).astype(BF16)
+
+    axial_mix = mixing(0, axial_c[...])
+    plane_mix = mixing(1, mix_c[...])
+    side_mix = mixing(2, mix_c[...])
+
+    convected = dot(plane_mix, u).astype(BF16)
+    plane_pattern = pattern_of(0.5 * plane_damp[0].astype(F32))
+    high = min(256, cells)
+    band = lax.broadcasted_iota(jnp.int32, (high, 128), 0).astype(F32).astype(BF16)
+    one = jnp.ones((high, 128), BF16)
+    zero = jnp.zeros((high, 128), BF16)
+
+    def build(first, count):
+        for at in range(first, first + count, 128):
+            for low in range(0, cells, high):
+                hits = []
+                for side in range(2):
+                    place = faces[side : side + 1, at : at + 128] - low
+                    place = jnp.clip(place, -1, high).astype(F32).astype(BF16)
+                    hits.append(jnp.where(band == place, one, zero))
+                plus[low : low + high, at : at + 128] = hits[0] + hits[1]
+                signed[low : low + high, at : at + 128] = hits[0] - hits[1]
+
+    def gather(first, count):
+        here = slice(first, first + count)
+        damped = by_layer(dot(u, signed[:, here]), plane_pattern[:, here])
+        flux[:, here] = (dot(convected, plus[:, here]) + damped).astype(BF16)
+
+    part = 256
+    starts = list(range(0, n_faces, part))
+    early = len(starts) // 2
+    build(0, part)
+    for at in starts[:early]:
+        build(at + part, part)
+        gather(at, part)
 
     pl.semaphore_wait(barrier, n_cell - 1 + n_circ - 1)
     copies = []
@@ -238,28 +261,10 @@
         for j in range(1, n_cell)
     ]
 
-    mix_high, mix_low = mixing(1, mix_c[...], False)
-    convected = (dot(mix_high, u) + dot(mix_low, u)).astype(BF16)
-    for q in range(cells // chunk):
-        ends = []
-        for side in range(2):
-            low = jnp.clip(faces[side : side + 1, :] - q * chunk, -1, chunk)
-            low = low.astype(F32).astype(BF16)
-            ends.append(jnp.broadcast_to(low, (step_rows, n_faces)))
-
-        def build(i, carry, q=q, ends=ends):
-            base = lax.broadcasted_iota(jnp.int32, (step_rows, n_faces), 0) + i * step_rows
-            base = base.astype(F32).astype(BF16)
-            one = jnp.ones((step_rows, n_faces), BF16)
-            zero = jnp.zeros((step_rows, n_faces), BF16)
-            owner = jnp.where(base == ends[0], one, zero)
-            other = jnp.where(base == ends[1], one, zero)
-            start = pl.multiple_of(q * chunk + i * step_rows, step_rows)
-            plus[pl.ds(start, step_rows), :] = owner + other
-            signed[pl.ds(start, step_rows), :] = owner - other
-            return carry
-
-        lax.fori_loop(0, chunk // step_rows, build, 0, unroll=2)
+    for at in starts[early:]:
+        if at + part < n_faces:
+            build(at + part, part)
+        gather(at, part)
 
     for copy in first:
         copy.wait_recv()
@@ -267,23 +272,15 @@
     for j in range(1, n_cell):
         summed = summed + forces_1[j]
     forces_2[0] = summed
-
-    plane_pattern = pattern_of(0.5 * plane_damp[0].astype(F32))
-    flux = dot(convected, plus[...]) + by_layer(dot(u, signed[...]), plane_pattern)
+    total[...] = lax.dot_general(flux[...], signed[...], NT, preferred_element_type=F32)
     second = [
         send(forces_2.at[0], forces_2.at[j], f2_send.at[j], f2_recv.at[j], circ_at(j))
         for j in range(1, n_circ)
     ]
-    total[...] = lax.dot_general(flux.astype(BF16), signed[...], NT, preferred_element_type=F32)
-
-    shapes_pad[...] = jnp.zeros_like(shapes_pad)
-    for part in range(2):
-        for d in range(n_circ):
-            at = (part * n_circ + d) * 8
-            shapes_pad[at : at + walls_k, :] = mode_shapes[part, d]
-    by_passage = jnp.dot(modes_c[...], shapes_pad[...], precision=HI, preferred_element_type=F32)
-
-    axial_high, axial_low = mixing(0, axial_c[...], True)
+
+    shapes = mode_shapes[...].reshape(2 * walls_k * n_circ, mode_shapes.shape[3])
+    by_passage = jnp.dot(modes_c[...], shapes, precision=HI, preferred_element_type=F32)
+
     to_below.wait_recv()
     to_above.wait_recv()
     stack[0:padded, :] = u
@@ -299,15 +296,12 @@
     below_damp = jnp.where(me_cell == 0, 0.0, below_damp)
     held = stack[...]
     derived = dot(fixed_c[...], held)
-    result = by_layer(
-        derived[0:padded] + derived[padded : 2 * padded], pattern_of(time_coef[0])
-    )
-    result = result - by_layer(derived[2 * padded : 3 * padded], pattern_of(0.5 * damp))
+    result = by_layer(derived[0:padded], pattern_of(time_coef[0] * (1.0 / scale)))
+    result = result - by_layer(derived[padded : 2 * padded], pattern_of(0.5 * damp))
     lower_damp = jnp.concatenate([below_damp, damp[0 : layers - 1]], axis=0)
-    result = result - by_layer(derived[3 * padded :], pattern_of(0.5 * lower_damp))
-    result = result + dot(axial_high, held) + dot(axial_low, held)
-
-    side_high, side_low = mixing(2, mix_c[...], False)
+    result = result - by_layer(derived[2 * padded :], pattern_of(0.5 * lower_damp))
+    result = result + dot(axial_mix, held)
+
     to_prev.wait_recv()
     to_next.wait_recv()
     left = lax.broadcasted_iota(jnp.int32, (padded, 2 * per), 1) < per
@@ -318,14 +312,15 @@
     upper = jnp.where(left, ahead, own_side)
     side_s = 0.5 * jnp.where(left[0:8], side_pattern, back_damp)
     lower_b, upper_b = lower.astype(BF16), upper.astype(BF16)
-    side_flux = dot(side_high, lower_b) + dot(side_high, upper_b)
-    side_flux = side_flux + dot(side_low, lower_b) + dot(side_low, upper_b)
+    side_flux = dot(side_mix, lower_b) + dot(side_mix, upper_b)
     side_flux = side_flux - by_layer(upper - lower, side_s)
     side_flux = jnp.where(left, side_flux, -side_flux).astype(BF16)
     result = result + lax.dot_general(
         side_flux, extra[:, n_walls:], NT, preferred_element_type=F32
     )
-    image[...] = (result + total[...]).astype(BF16)
+    result = result + total[...]
+    for r in range(n_rows):
+        image[r] = result[r * layers : (r + 1) * layers].astype(BF16)
 
     for copy in second:
         copy.wait_recv()
@@ -350,22 +345,23 @@
     per = face_map.shape[0]
     n_faces = face_cells.shape[1]
     n_walls = wall_cells.shape[0]
-    fixed = constants(layers, n_circ, walls_k)
-    rows = HB * NV * layers
+    fixed, scale = constants(layers, n_circ, walls_k)
     padded = fixed[0].shape[0]
     side = fixed[3].shape[0] // 2
-    lanes = fixed[6].shape[0]
-    state = jnp.pad(flow_state.reshape(rows, cells), ((0, padded - rows), (0, 0)))
+    lanes = fixed[7].shape[0]
+    state = flow_state.reshape(HB * NV, layers, cells)
     vmem = pl.BlockSpec(memory_space=pltpu.VMEM)
     smem = pl.BlockSpec(memory_space=pltpu.SMEM)
     dma = pltpu.SemaphoreType.DMA
     image, modal = pl.pallas_call(
-        functools.partial(kernel, n_cell=n_cell, n_circ=n_circ, layers=layers),
+        functools.partial(
+            kernel, n_cell=n_cell, n_circ=n_circ, layers=layers, padded=padded, scale=scale
+        ),
         out_shape=(
-            jax.ShapeDtypeStruct((padded, cells), BF16),
+            jax.ShapeDtypeStruct((HB * NV, layers, cells), BF16),
             jax.ShapeDtypeStruct((HB, n_modes), F32),
         ),
-        in_specs=[vmem] * 5 + [smem] + [vmem] * 5 + [smem] + [vmem] * 8,
+        in_specs=[vmem] * 11 + [smem] + [vmem] * 9,
         out_specs=(vmem, vmem),
         scratch_shapes=[
             pltpu.VMEM((cells, n_walls + 2 * per), BF16),
@@ -380,18 +376,18 @@
             pltpu.VMEM((padded + 16, 2 * per), BF16),
             pltpu.VMEM((n_cell, 8, lanes), F32),
             pltpu.VMEM((n_circ, 8, lanes), F32),
-            pltpu.VMEM((2 * n_circ * 8, n_modes), F32),
+            pltpu.VMEM((padded, n_faces), BF16),
             pltpu.VMEM((padded, cells), F32),
             dma((2,)), dma((2,)), dma((2,)), dma((2,)),
             dma((n_cell,)), dma((n_cell,)), dma((n_circ,)), dma((n_circ,)),
         ],
         compiler_params=pltpu.CompilerParams(collective_id=0, has_side_effects=True),
     )(
-        state, time_coef, axial_damp, plane_damp, periodic_damp, flux_jacobian, face_cells,
-        periodic_cells, face_map[None], wall_cells[None], wall_normals, pressure_weights,
-        mode_shapes, *fixed,
-    )
-    return image[:rows].reshape(HB * NV, 1, layers, cells), modal
+        state, time_coef, axial_damp, plane_damp, periodic_damp,
+        flux_jacobian.transpose(1, 0, 2), face_cells, periodic_cells, face_map[None], wall_cells[None], wall_normals, pressure_weights,
+        mode_shapes.transpose(0, 2, 1, 3), *fixed,
+    )
+    return image.reshape(HB * NV, 1, layers, cells), modal
 
 
 def solution(mesh):

time: 25.8 us -> 23.6 us (0.915)
  local copies, waits for them, and re-layouts: 7.08 us -> 2.38 us
  Pallas kernels: 17.8 us -> 20.4 us
    reshape x2 -> x0, local copies, waits for them, and re-layouts: 2.82 us -> none  [the longest x1 1.8 us: shards(): return (image[:rows].reshape(HB * NV, 1, layers, cells), modal)]
    pallas_call x1, Pallas kernels: 17.8 us -> 20.4 us  [shards(): pl.pallas_call(functools.partial(kernel, n_cell=n_cell, n_circ=n_circ, la...]
    unnamed x5 -> x4, local copies, waits for them, and re-layouts: 3.53 us -> 2.38 us
    pad x1 -> x0, local copies, waits for them, and re-layouts: 0.73 us -> none  [shards(): jnp.pad(flow_state.reshape(rows, cells), ((0, padded - rows), (0, 0)))]
where the time goes in v2:
time: 23.6 us; the launch traced here: 23.5 us
  Pallas kernels  20.4 us (86%)
  local copies, waits for them, and re-layouts  2.38 us (10%)
  between operations  0.65 us (3%)
    pallas_call x1, Pallas kernels, shards(): pl.pallas_call(functools.partial(kernel, n_cell=n_cell, n_circ=n_circ, la...  20.4 us
    unnamed x4, local copies, waits for them, and re-layouts  2.38 us

profile of v2, /device:TPU:0, one launch (start us, length us, event | category | flops | bytes accessed | tf_op | source)
XLA Modules:
  0.0 23.5 jit_solution(14515481163922810590)
XLA Ops:
  0.6 20.4 %shard_map.212 = (bf16[35,4,1024]{2,1,0:T(4,128)(2,1)}, f32[7,400]{1,0:T(8,128)}) custom-call(bf16[35,4,1024]{2,1,0:T(4,128)(2,1)} %bitcast.8, f32[1,4,1024]{2,1,0:T(4,128)} %time_coef.1, bf16[1,4,1024]{2,1,0:T(4,128)(2,1)} %axial_damp.1, bf16[1,4,2048]{2,1,0:T(4,128)(2,1)} %plane_damp.1, bf16[1,4,64]{2,1,0:T(4,128)(2,1)} %periodic_damp.1, ...), custom_call_target="tpu_custom_call" | custom-call | tf_op jit(solution)/shard_map/pallas_call | solution.py:356
  21.1 0.0 copy-start
  21.1 1.8 %copy.26 = bf16[35,1,4,1024]{3,2,1,0:T(4,128)(2,1)} copy(bf16[35,1,4,1024]{3,2,1,0:T(4,128)(2,1)} %bitcast.9) | data formatting | bytes 573440
  22.9 0.0 copy-done
  22.9 0.6 %copy.27 = f32[7,400]{1,0:T(8,128)} copy(f32[7,400]{1,0:T(8,128)S(1)} %copy-done) | data formatting | bytes 22400
Async XLA Ops:
  21.1 1.8 %copy-start = (f32[7,400]{1,0:T(8,128)S(1)}, f32[7,400]{1,0:T(8,128)}, u32[]{:S(2)}) copy-start(f32[7,400]{1,0:T(8,128)} %get-tuple-element.11) | copy-start | bytes 33604

commit v3 on v2

--- a/solution.py
+++ b/solution.py
@@ -152,27 +152,37 @@
     wall_layer = lax.div(wall_index, cells)
     wall_column = wall_index - wall_layer * cells
     columns = jnp.concatenate([wall_column, sides[1:2, :], targets], axis=1)
-    chunk = 256
-    step_rows = 16
-    for q in range(cells // chunk):
-        low = jnp.clip(columns - q * chunk, -1, chunk).astype(F32).astype(BF16)
-        low = jnp.broadcast_to(low, (step_rows, low.shape[1]))
-
-        def fill(i, carry, q=q, low=low):
-            base = lax.broadcasted_iota(jnp.int32, low.shape, 0) + i * step_rows
-            hit = base.astype(F32).astype(BF16) == low
-            start = pl.multiple_of(q * chunk + i * step_rows, step_rows)
-            extra[pl.ds(start, step_rows), :] = jnp.where(hit, 1.0, 0.0).astype(BF16)
-            return carry
-
-        lax.fori_loop(0, chunk // step_rows, fill, 0, unroll=4)
+    high = min(256, cells)
+    piece = 32
+    bands = [
+        (lax.broadcasted_iota(jnp.int32, (piece, 128), 0) + start).astype(F32).astype(BF16)
+        for start in range(0, high, piece)
+    ]
+    one = jnp.ones((piece, 128), BF16)
+    zero = jnp.zeros((piece, 128), BF16)
+
+    def places(row, low):
+        place = jnp.clip(row - low, -1, high).astype(F32).astype(BF16)
+        return jnp.broadcast_to(place, (piece, 128))
+
+    for at in range(extra.shape[0]):
+        row = columns[:, at * 128 : (at + 1) * 128]
+        for low in range(0, cells, high):
+            place = places(row, low)
+            for k, band in enumerate(bands):
+                start = low + k * piece
+                extra[at, start : start + piece, :] = jnp.where(band == place, one, zero)
+
+    def tiles(table, first, count):
+        found = [table[first // 128 + k] for k in range(count // 128)]
+        return jnp.concatenate(found, axis=1)
 
     cell_out[0 : 2 * side_rows, :] = dot(pick_c[...], u).astype(BF16)
     damp = axial_damp[0].astype(F32)
     last = damp[layers - 1 : layers]
     cell_out[2 * side_rows :, :] = jnp.broadcast_to(last, (16, cells)).astype(BF16)
 
-    gathered = dot(u, extra[...])
+    gathered = dot(u, tiles(extra, 0, n_walls + 2 * per))
     own_side = gathered[:, n_walls:]
     side_out[0:padded, :] = own_side.astype(BF16)
     side_damp = periodic_damp[0].astype(F32)
@@ -205,26 +215,22 @@
 
     convected = dot(plane_mix, u).astype(BF16)
     plane_pattern = pattern_of(0.5 * plane_damp[0].astype(F32))
-    high = min(256, cells)
-    band = lax.broadcasted_iota(jnp.int32, (high, 128), 0).astype(F32).astype(BF16)
-    one = jnp.ones((high, 128), BF16)
-    zero = jnp.zeros((high, 128), BF16)
 
     def build(first, count):
         for at in range(first, first + count, 128):
+            rows = [faces[side : side + 1, at : at + 128] for side in range(2)]
             for low in range(0, cells, high):
-                hits = []
-                for side in range(2):
-                    place = faces[side : side + 1, at : at + 128] - low
-                    place = jnp.clip(place, -1, high).astype(F32).astype(BF16)
-                    hits.append(jnp.where(band == place, one, zero))
-                plus[low : low + high, at : at + 128] = hits[0] + hits[1]
-                signed[low : low + high, at : at + 128] = hits[0] - hits[1]
+                owner, other = places(rows[0], low), places(rows[1], low)
+                for k, band in enumerate(bands):
+                    start = low + k * piece
+                    hit = jnp.where(band == owner, one, jnp.where(band == other, -one, zero))
+                    plus[at // 128, start : start + piece, :] = jnp.abs(hit)
+                    signed[at // 128, start : start + piece, :] = hit
 
     def gather(first, count):
         here = slice(first, first + count)
-        damped = by_layer(dot(u, signed[:, here]), plane_pattern[:, here])
-        flux[:, here] = (dot(convected, plus[:, here]) + damped).astype(BF16)
+        damped = by_layer(dot(u, tiles(signed, first, count)), plane_pattern[:, here])
+        flux[:, here] = (dot(convected, tiles(plus, first, count)) + damped).astype(BF16)
 
     part = 256
     starts = list(range(0, n_faces, part))
@@ -272,14 +278,17 @@
     for j in range(1, n_cell):
         summed = summed + forces_1[j]
     forces_2[0] = summed
-    total[...] = lax.dot_general(flux[...], signed[...], NT, preferred_element_type=F32)
+    shapes = mode_shapes[...].reshape(2 * walls_k * n_circ, mode_shapes.shape[3])
+    by_passage = jnp.dot(modes_c[...], shapes, precision=HI, preferred_element_type=F32)
+
     second = [
         send(forces_2.at[0], forces_2.at[j], f2_send.at[j], f2_recv.at[j], circ_at(j))
         for j in range(1, n_circ)
     ]
 
-    shapes = mode_shapes[...].reshape(2 * walls_k * n_circ, mode_shapes.shape[3])
-    by_passage = jnp.dot(modes_c[...], shapes, precision=HI, preferred_element_type=F32)
+    total[...] = lax.dot_general(
+        flux[...], tiles(signed, 0, n_faces), NT, preferred_element_type=F32
+    )
 
     to_below.wait_recv()
     to_above.wait_recv()
@@ -316,7 +325,7 @@
     side_flux = side_flux - by_layer(upper - lower, side_s)
     side_flux = jnp.where(left, side_flux, -side_flux).astype(BF16)
     result = result + lax.dot_general(
-        side_flux, extra[:, n_walls:], NT, preferred_element_type=F32
+        side_flux, tiles(extra, n_walls, 2 * per), NT, preferred_element_type=F32
     )
     result = result + total[...]
     for r in range(n_rows):
@@ -331,6 +340,17 @@
     modal[...] = answer[0:HB]
     for copy in copies:
         copy.wait_send()
+
+
+def deliver(image, modal, image_out, modal_out, sems):
+    copies = [
+        pltpu.make_async_copy(image, image_out, sems.at[0]),
+        pltpu.make_async_copy(modal, modal_out, sems.at[1]),
+    ]
+    for copy in copies:
+        copy.start()
+    for copy in copies:
+        copy.wait()
 
 
 def shards(
@@ -364,9 +384,9 @@
         in_specs=[vmem] * 11 + [smem] + [vmem] * 9,
         out_specs=(vmem, vmem),
         scratch_shapes=[
-            pltpu.VMEM((cells, n_walls + 2 * per), BF16),
-            pltpu.VMEM((cells, n_faces), BF16),
-            pltpu.VMEM((cells, n_faces), BF16),
+            pltpu.VMEM(((n_walls + 2 * per) // 128, cells, 128), BF16),
+            pltpu.VMEM((n_faces // 128, cells, 128), BF16),
+            pltpu.VMEM((n_faces // 128, cells, 128), BF16),
             pltpu.VMEM((padded + 2 * side, cells), BF16),
             pltpu.VMEM((2 * side + 16, cells), BF16),
             pltpu.VMEM((side, cells), BF16),
@@ -387,6 +407,17 @@
         flux_jacobian.transpose(1, 0, 2), face_cells, periodic_cells, face_map[None], wall_cells[None], wall_normals, pressure_weights,
         mode_shapes.transpose(0, 2, 1, 3), *fixed,
     )
+    anywhere = pl.BlockSpec(memory_space=pl.ANY)
+    image, modal = pl.pallas_call(
+        deliver,
+        out_shape=(
+            jax.ShapeDtypeStruct(image.shape, BF16),
+            jax.ShapeDtypeStruct(modal.shape, F32),
+        ),
+        in_specs=[anywhere] * 2,
+        out_specs=(vmem, vmem),
+        scratch_shapes=[dma((2,))],
+    )(image, modal)
     return image.reshape(HB * NV, 1, layers, cells), modal
 
 

time: 23.6 us -> 20.6 us (0.87)
  local copies, waits for them, and re-layouts: 2.38 us -> 0 us
  Pallas kernels: 20.4 us -> 19.8 us
    unnamed x4 -> x0, local copies, waits for them, and re-layouts: 2.38 us -> none
    pallas_call x1, Pallas kernels: 20.4 us -> 18.1 us  [shards(): pl.pallas_call(functools.partial(kernel, n_cell=n_cell, n_circ=n_circ, la...]
    pallas_call x0 -> x1, Pallas kernels: none -> 1.69 us  [shards(): pl.pallas_call(deliver, out_shape=(jax.ShapeDtypeStruct(image.shape, BF16...]
where the time goes in v3:
time: 20.6 us; the launch traced here: 20.5 us
  Pallas kernels  19.8 us (96%)
  between operations  0.64 us (3%)
    pallas_call x1, Pallas kernels, shards(): pl.pallas_call(functools.partial(kernel, n_cell=n_cell, n_circ=n_circ, la...  18.1 us
    pallas_call x1, Pallas kernels, shards(): pl.pallas_call(deliver, out_shape=(jax.ShapeDtypeStruct(image.shape, BF16...  1.69 us

profile of v3, /device:TPU:0, one launch (start us, length us, event | category | flops | bytes accessed | tf_op | source)
XLA Modules:
  0.0 20.5 jit_solution(15730525692523374513)
XLA Ops:
  0.6 18.1 %shard_map.212 = (bf16[35,4,1024]{2,1,0:T(4,128)(2,1)}, f32[7,400]{1,0:T(8,128)}) custom-call(bf16[35,4,1024]{2,1,0:T(4,128)(2,1)} %bitcast.8, f32[1,4,1024]{2,1,0:T(4,128)} %time_coef.1, bf16[1,4,1024]{2,1,0:T(4,128)(2,1)} %axial_damp.1, bf16[1,4,2048]{2,1,0:T(4,128)(2,1)} %plane_damp.1, bf16[1,4,64]{2,1,0:T(4,128)(2,1)} %periodic_damp.1, ...), custom_call_target="tpu_custom_call" | custom-call | tf_op jit(solution)/shard_map/pallas_call | solution.py:376
  18.8 1.7 %shard_map.213 = (bf16[35,4,1024]{2,1,0:T(4,128)(2,1)}, f32[7,400]{1,0:T(8,128)}) custom-call(bf16[35,4,1024]{2,1,0:T(4,128)(2,1)} %get-tuple-element.6.image, f32[7,400]{1,0:T(8,128)} %get-tuple-element.7.modal), custom_call_target="tpu_custom_call" | custom-call | tf_op jit(solution)/shard_map/pallas_call | solution.py:411

commit v4 on v3

--- a/solution.py
+++ b/solution.py
@@ -105,7 +105,7 @@
     wall_cells, normals, press_w, mode_shapes,
     mix_c, axial_c, fixed_c, pick_c, weights_c, of_row_c, of_column_c, modes_c,
     image, modal,
-    extra, plus, signed, stack, cell_out, above, below, side_out, side_next, side_prev,
+    extra, signed, stack, cell_out, above, below, side_out, side_next, side_prev,
     forces_1, forces_2, flux, total,
     cell_send, cell_recv, side_send, side_recv, f1_send, f1_recv, f2_send, f2_recv,
     *, n_cell, n_circ, layers, padded, scale,
@@ -224,13 +224,13 @@
                 for k, band in enumerate(bands):
                     start = low + k * piece
                     hit = jnp.where(band == owner, one, jnp.where(band == other, -one, zero))
-                    plus[at // 128, start : start + piece, :] = jnp.abs(hit)
                     signed[at // 128, start : start + piece, :] = hit
 
     def gather(first, count):
         here = slice(first, first + count)
-        damped = by_layer(dot(u, tiles(signed, first, count)), plane_pattern[:, here])
-        flux[:, here] = (dot(convected, tiles(plus, first, count)) + damped).astype(BF16)
+        table = tiles(signed, first, count)
+        damped = by_layer(dot(u, table), plane_pattern[:, here])
+        flux[:, here] = (dot(convected, jnp.abs(table)) + damped).astype(BF16)
 
     part = 256
     starts = list(range(0, n_faces, part))
@@ -267,24 +267,28 @@
         for j in range(1, n_cell)
     ]
 
-    for at in starts[early:]:
-        if at + part < n_faces:
-            build(at + part, part)
-        gather(at, part)
-
+    def chunks(some):
+        for at in some:
+            if at + part < n_faces:
+                build(at + part, part)
+            gather(at, part)
+
+    joined = early + (len(starts) - early) // 2
+    chunks(starts[early:joined])
     for copy in first:
         copy.wait_recv()
     summed = forces_1[0]
     for j in range(1, n_cell):
         summed = summed + forces_1[j]
     forces_2[0] = summed
-    shapes = mode_shapes[...].reshape(2 * walls_k * n_circ, mode_shapes.shape[3])
-    by_passage = jnp.dot(modes_c[...], shapes, precision=HI, preferred_element_type=F32)
-
+    chunks(starts[joined : joined + 1])
     second = [
         send(forces_2.at[0], forces_2.at[j], f2_send.at[j], f2_recv.at[j], circ_at(j))
         for j in range(1, n_circ)
     ]
+    chunks(starts[joined + 1 :])
+    shapes = mode_shapes[...].reshape(2 * walls_k * n_circ, mode_shapes.shape[3])
+    by_passage = jnp.dot(modes_c[...], shapes, precision=HI, preferred_element_type=F32)
 
     total[...] = lax.dot_general(
         flux[...], tiles(signed, 0, n_faces), NT, preferred_element_type=F32
@@ -386,7 +390,6 @@
         scratch_shapes=[
             pltpu.VMEM(((n_walls + 2 * per) // 128, cells, 128), BF16),
             pltpu.VMEM((n_faces // 128, cells, 128), BF16),
-            pltpu.VMEM((n_faces // 128, cells, 128), BF16),
             pltpu.VMEM((padded + 2 * side, cells), BF16),
             pltpu.VMEM((2 * side + 16, cells), BF16),
             pltpu.VMEM((side, cells), BF16),

time: 20.6 us -> 20 us (0.971)
  Pallas kernels: 19.8 us -> 19.2 us
    pallas_call x1, Pallas kernels: 18.1 us -> 17.5 us  [shards(): pl.pallas_call(functools.partial(kernel, n_cell=n_cell, n_circ=n_circ, la...]
where the time goes in v4:
time: 20 us; the launch traced here: 19.8 us
  Pallas kernels  19.2 us (96%)
  between operations  0.64 us (3%)
    pallas_call x1, Pallas kernels, shards(): pl.pallas_call(functools.partial(kernel, n_cell=n_cell, n_circ=n_circ, la...  17.5 us
    pallas_call x1, Pallas kernels, shards(): pl.pallas_call(deliver, out_shape=(jax.ShapeDtypeStruct(image.shape, BF16...  1.69 us

profile of v4, /device:TPU:0, one launch (start us, length us, event | category | flops | bytes accessed | tf_op | source)
XLA Modules:
  0.0 19.8 jit_solution(13010738530761595523)
XLA Ops:
  0.6 17.5 %shard_map.212 = (bf16[35,4,1024]{2,1,0:T(4,128)(2,1)}, f32[7,400]{1,0:T(8,128)}) custom-call(bf16[35,4,1024]{2,1,0:T(4,128)(2,1)} %bitcast.8, f32[1,4,1024]{2,1,0:T(4,128)} %time_coef.1, bf16[1,4,1024]{2,1,0:T(4,128)(2,1)} %axial_damp.1, bf16[1,4,2048]{2,1,0:T(4,128)(2,1)} %plane_damp.1, bf16[1,4,64]{2,1,0:T(4,128)(2,1)} %periodic_damp.1, ...), custom_call_target="tpu_custom_call" | custom-call | tf_op jit(solution)/shard_map/pallas_call | solution.py:380
  18.1 1.7 %shard_map.213 = (bf16[35,4,1024]{2,1,0:T(4,128)(2,1)}, f32[7,400]{1,0:T(8,128)}) custom-call(bf16[35,4,1024]{2,1,0:T(4,128)(2,1)} %get-tuple-element.6.image, f32[7,400]{1,0:T(8,128)} %get-tuple-element.7.modal), custom_call_target="tpu_custom_call" | custom-call | tf_op jit(solution)/shard_map/pallas_call | solution.py:414
